TPU v7x, 32 devices: a whole 2x2x4 slice. The times are simulated.
32 devices in a mesh: corpus: 4 (over y, x), fsdp: 8 (over z, core).
Axes of the slice: x: 2, y: 2, z: 4, core: 2. Of those that a mesh axis runs over, the one named last changes fastest.
Arguments:
- inputs: bfloat16 [2048, 4096], P('fsdp', 'corpus'), may hold values from -128 to 128
- norm_gain: float32 [4096], replicated, may hold values from 0.1 to 1.9
- w_query: bfloat16 [4096, 8192], P('fsdp', 'corpus'), may hold values from -0.09375 to 0.09375
- w_key: bfloat16 [4096, 1024], P('fsdp', 'corpus'), may hold values from -0.09375 to 0.09375
- w_value: bfloat16 [4096, 1024], P('fsdp', 'corpus'), may hold values from -0.375 to 0.375
- query_bias: float32 [8192], P('corpus'), may hold values from -16 to 16
- key_bias: float32 [1024], P('corpus'), may hold values from -16 to 16
- value_bias: float32 [1024], P('corpus'), may hold values from -4 to 4
- key_cache: bfloat16 [8, 2048, 1024], P('fsdp', None, 'corpus'), may hold values from -16 to 16
- value_cache: bfloat16 [8, 2048, 1024], P('fsdp', None, 'corpus'), may hold values from -16 to 16
- source_doc: int32 [32], P('fsdp'), may hold values from 0 to 7, as said below
- prefix_len: int32 [32], P('fsdp'), may hold values from 1 to 2048
Outputs:
- attention: bfloat16 [2048, 8192], P('fsdp', 'corpus')
Inputs may be any that keep to these rules, and one draw needn't show every extreme that they name: `source_doc`: within the suffixes of one index of fsdp (aligned blocks of 4) no document appears more than 2 times, and one document, drawn from the seed, appears exactly 2 times in every such block.
All inputs are finite; a program needn't handle non-finite values.
Results may differ from a plain program's by a relative error of at most 0.0075.
The roundings to bfloat16 on the way count: a program that leaves them out, or rounds other values in their place, can miss the bound.
Values may be sent and summed in bfloat16 or wider, within the bound.
A program may use at most 128 MiB of HBM per device.

v0:
```python
import jax
import jax.numpy as jnp
from jax import lax
from jax.sharding import PartitionSpec as P

HD = 128
SL = 64
CAP = 2
EPS = 1e-06
THETA = 1000000.0
MASKED = -1e30


def rope_tables(position, width):
    half = width // 2
    freq = THETA ** (-(jnp.arange(half, dtype=jnp.float32) * 2.0 / width))
    angle = position.astype(jnp.float32)[..., None] * freq
    angle = jnp.concatenate([angle, angle], axis=-1)
    return (jnp.cos(angle), jnp.sin(angle))


def rotate(vector, cosine, sine):
    half = vector.shape[-1] // 2
    turned = jnp.concatenate([-vector[..., half:], vector[..., :half]], axis=-1)
    return vector * cosine + turned * sine


def normalize(rows, norm_gain):
    wide = rows.astype(jnp.float32)
    spread = jnp.mean(wide * wide, axis=-1, keepdims=True)
    return (wide * lax.rsqrt(spread + EPS) * norm_gain).astype(jnp.bfloat16)


def partial_attend(query, keys, values, live):
    count = query.shape[0]
    width = query.shape[2]
    length = keys.shape[0]
    kv_heads = keys.shape[1] // width
    group = query.shape[1] // kv_heads
    grouped = query.reshape(count, kv_heads, group, width)
    key_rows = keys.reshape(length, kv_heads, width)
    scores = jnp.einsum(
        "tkgd,lkd->tkgl", grouped, key_rows, preferred_element_type=jnp.float32
    ) * width ** (-0.5)
    scores = jnp.where(live[:, None, None, :], scores, MASKED)
    peak = jnp.max(scores, axis=-1)
    weights = jnp.exp(scores - peak[..., None])
    total = jnp.sum(weights, axis=-1)
    rounded = weights.astype(jnp.bfloat16)
    value_rows = values.reshape(length, kv_heads, width)
    weighted = jnp.einsum("tkgl,lkd->tkgd", rounded, value_rows, preferred_element_type=jnp.float32)
    return (
        weighted.reshape(count, kv_heads * group * width),
        peak.reshape(count, kv_heads * group),
        total.reshape(count, kv_heads * group),
    )


def settle(part):
    weighted, peak, total = part
    shape = peak.shape + (-1,)
    normed = (
        (weighted.reshape(shape) / total[..., None]).reshape(weighted.shape).astype(jnp.bfloat16)
    )
    return (normed, peak + jnp.log(total))


def combine(prefix_normed, prefix_lse, own):
    own_out, own_peak, own_total = own
    top = jnp.maximum(prefix_lse, own_peak)
    scale_first = jnp.exp(prefix_lse - top)
    scale_second = jnp.exp(own_peak - top)
    divisor = scale_first + own_total * scale_second
    shape = own_peak.shape + (-1,)
    mixed = (
        prefix_normed.astype(jnp.float32).reshape(shape) * scale_first[..., None]
        + own_out.reshape(shape) * scale_second[..., None]
    )
    mixed = mixed / divisor[..., None]
    return mixed.reshape(own_peak.shape[:-1] + (-1,)).astype(jnp.bfloat16)


def shards(
    inputs,
    norm_gain,
    w_query,
    w_key,
    w_value,
    query_bias,
    key_bias,
    value_bias,
    key_cache,
    value_cache,
    source_doc,
    prefix_len,
):
    full_rows = lax.all_gather(inputs, "corpus", axis=1, tiled=True)
    normed = normalize(full_rows, norm_gain)
    query_lin = jnp.dot(
        normed,
        lax.all_gather(w_query, "fsdp", axis=0, tiled=True),
        preferred_element_type=jnp.float32,
    )
    key_lin = jnp.dot(
        normed,
        lax.all_gather(w_key, "fsdp", axis=0, tiled=True),
        preferred_element_type=jnp.float32,
    )
    value_lin = jnp.dot(
        normed,
        lax.all_gather(w_value, "fsdp", axis=0, tiled=True),
        preferred_element_type=jnp.float32,
    )
    suffixes = source_doc.shape[0]
    width = HD
    q_heads = w_query.shape[1] // width
    kv_heads = w_key.shape[1] // width
    position = prefix_len[:, None] + jnp.arange(SL, dtype=jnp.int32)[None, :]
    cosine, sine = rope_tables(position, width)
    cosine = cosine[:, :, None, :]
    sine = sine[:, :, None, :]
    queries = rotate(
        (query_lin + query_bias).reshape(suffixes, SL, q_heads, width), cosine, sine
    ).astype(jnp.bfloat16)
    own_keys = rotate(
        (key_lin + key_bias).reshape(suffixes, SL, kv_heads, width), cosine, sine
    ).astype(jnp.bfloat16)
    own_keys = own_keys.reshape(suffixes, SL, kv_heads * width)
    own_values = (
        (value_lin + value_bias).astype(jnp.bfloat16).reshape(suffixes, SL, kv_heads * width)
    )
    causal = jnp.arange(SL, dtype=jnp.int32)[None, :] <= jnp.arange(SL, dtype=jnp.int32)[:, None]
    own_part = jax.vmap(partial_attend, in_axes=(0, 0, 0, None))(
        queries, own_keys, own_values, causal
    )
    documents = lax.axis_size("fsdp")
    slots = documents * CAP
    doc_length = key_cache.shape[1]
    order = jnp.arange(suffixes, dtype=jnp.int32)
    earlier = (source_doc[None, :] == source_doc[:, None]) & (order[None, :] < order[:, None])
    ranking = jnp.sum(earlier.astype(jnp.int32), axis=1)
    slot_of = source_doc * CAP + ranking
    matches = slot_of[None, :] == jnp.arange(slots, dtype=jnp.int32)[:, None]
    holder = jnp.sum(jnp.where(matches, order[None, :], 0), axis=1)
    occupied = jnp.any(matches, axis=1)
    slot_length = jnp.where(occupied, jnp.take(prefix_len, holder, axis=0), 0)
    slot_mask = (jnp.arange(doc_length, dtype=jnp.int32)[None, :] < slot_length[:, None]).astype(
        jnp.bfloat16
    )
    slot_queries = jnp.take(queries, holder, axis=0)
    initial = (
        jnp.zeros((suffixes, SL, q_heads * width), jnp.float32),
        jnp.zeros((suffixes, SL, q_heads), jnp.float32),
        jnp.zeros((suffixes, SL, q_heads), jnp.float32),
    )
    key_piece = lax.all_gather(key_cache, "fsdp", axis=0, tiled=True)
    value_piece = lax.all_gather(value_cache, "fsdp", axis=0, tiled=True)
    count = key_piece.shape[0]

    def one_document(item):
        doc_queries, doc_masks, doc_keys, doc_values = item
        live = jnp.broadcast_to(doc_masks[:, None, :] > 0, (CAP, SL, doc_masks.shape[-1]))
        return jax.vmap(partial_attend, in_axes=(0, None, None, 0))(
            doc_queries, doc_keys, doc_values, live
        )

    results = lax.map(
        one_document,
        (
            slot_queries.reshape((count, CAP) + slot_queries.shape[1:]),
            slot_mask.reshape(count, CAP, doc_length),
            key_piece,
            value_piece,
        ),
    )
    results = tuple((part.reshape((count * CAP,) + part.shape[2:]) for part in results))
    inside = (slot_of >= 0) & (slot_of < count * CAP)
    chosen = jnp.clip(slot_of, 0, count * CAP - 1)
    gathered_part = tuple(
        (
            jnp.where(inside[:, None, None], jnp.take(fresh, chosen, axis=0), older)
            for older, fresh in zip(initial, results)
        )
    )
    prefix_normed, prefix_lse = settle(gathered_part)
    attention = combine(prefix_normed, prefix_lse, own_part)
    return attention.reshape(suffixes * SL, q_heads * width)


def solution(mesh):
    in_specs = (
        P("fsdp", "corpus"),
        P(),
        P("fsdp", "corpus"),
        P("fsdp", "corpus"),
        P("fsdp", "corpus"),
        P("corpus"),
        P("corpus"),
        P("corpus"),
        P("fsdp", None, "corpus"),
        P("fsdp", None, "corpus"),
        P("fsdp"),
        P("fsdp"),
    )
    out_specs = P("fsdp", "corpus")
    return jax.shard_map(shards, mesh=mesh, in_specs=in_specs, out_specs=out_specs, check_vma=False)
```

profile of v0, /device:TPU:0, one launch (start us, length us, event | category | flops | bytes accessed | tf_op | source)
XLA Modules:
  0.0 685.7 jit_solution(6007420988527938023)
XLA Ops:
  15.4 31.9 %all-gather.11.cloned.1.call-done = bf16[256,4096]{1,0:T(8,128)(2,1)} async-done(((bf16[256,1024]{1,0:T(8,128)(2,1)}), bf16[256,4096]{1,0:T(8,128)(2,1)}) %all-gather.11.cloned.1.call-update) | async-done | bytes 2097168 | tf_op jit(solution)/shard_map/all_gather | solution.py:97
  49.5 28.5 %all-gather.15.cloned.1.call-done = bf16[4096,256]{1,0:T(8,128)(2,1)} async-done(((bf16[512,256]{1,0:T(8,128)(2,1)}), bf16[4096,256]{1,0:T(8,128)(2,1)}) %all-gather.15.cloned.1.call-update) | async-done | bytes 2097168 | tf_op jit(solution)/shard_map/all_gather | solution.py:106
  80.5 27.7 %all-gather.17.cloned.1.call-done = bf16[4096,256]{1,0:T(8,128)(2,1)} async-done(((bf16[512,256]{1,0:T(8,128)(2,1)}), bf16[4096,256]{1,0:T(8,128)(2,1)}) %all-gather.17.cloned.1.call-update) | async-done | bytes 2097168 | tf_op jit(solution)/shard_map/all_gather | solution.py:111
  110.8 149.5 %all-gather.13.cloned.1.call-done = bf16[4096,2048]{1,0:T(8,128)(2,1)} async-done(((bf16[512,2048]{1,0:T(8,128)(2,1)}), bf16[4096,2048]{1,0:T(8,128)(2,1)}) %all-gather.13.cloned.1.call-update) | async-done | bytes 16777232 | tf_op jit(solution)/shard_map/all_gather | solution.py:101
  260.3 8.2 %fusion.26 = f32[32,8,16,128]{3,1,2,0:T(8,128)S(1)} fusion(bf16[4096,2048]{1,0:T(8,128)(2,1)} %all-gather.13.cloned.1.call-done, f32[2048]{0:T(1024)S(1)} %copy-done.18, bf16[256,4096]{1,0:T(8,128)(2,1)S(1)} %copy-done.7, f32[4096]{0:T(1024)S(1)} %copy-done.17, f32[256]{0:T(256)S(1)} %add_rsqrt_fusion), kind=kOutput, calls=%fused_computation.52 | convolution fusion | flops 4299685888 | bytes 20997120 | tf_op jit(solution)/shard_map/dot_general | solution.py:99
  291.7 50.4 %all-gather.9.cloned.1.call-done = bf16[8,2048,256]{2,1,0:T(8,128)(2,1)} async-done(((bf16[1,2048,256]{2,1,0:T(8,128)(2,1)}), bf16[8,2048,256]{2,1,0:T(8,128)(2,1)}) %all-gather.9.cloned.1.call-update) | async-done | bytes 8388624 | tf_op jit(solution)/shard_map/all_gather | solution.py:156
  342.1 82.1 %all-gather.7.cloned.1.call-done = bf16[8,2048,256]{2,1,0:T(8,128)(2,1)} async-done(((bf16[1,2048,256]{2,1,0:T(8,128)(2,1)}), bf16[8,2048,256]{2,1,0:T(8,128)(2,1)}) %all-gather.7.cloned.1.call-update) | async-done | bytes 8388624 | tf_op jit(solution)/shard_map/all_gather | solution.py:157
  424.2 241.4 %while.14 = (s32[]{:T(128)}, f32[8,2,64,2048]{3,2,1,0:T(8,128)}, f32[8,2,64,16]{2,3,1,0:T(8,128)S(1)}, f32[8,2,64,16]{2,3,1,0:T(8,128)S(1)}, bf16[8,2048,256]{2,...) while((s32[]{:T(128)}, f32[8,2,64,2048]{3,2,1,0:T(8,128)}, ...), condition=%wide.region_7.8_spmd, body=%wide.region_4.0_spmd.sunk | while | flops 2193620992 | bytes 74047632 | solution.py:167
  429.9 7.1 %fusion.71 = (f32[2,64,2,8]{1,3,0,2:T(8,128)S(1)}, f32[2,2048,2,64,8]{1,3,4,2,0:T(8,128)}) fusion(pred[2,2048]{1,0:T(4,128)(4,1)S(1)} %compare_bitcast_fusion.2, bf16[2048,2,128,1,1]{0,2,4,3,1:T(8,128)(2,1)S(1)} %bitcast.138, bf16[2,64,2,8,128]{4,3,2,1,0:T(8,128)(2,1)S(1)} %dynamic-slice_bitcast_fusion.2), kind=kOutput, calls=%fused_computation.9.clone.1 | convolution fusion | flops 1086322688 | bytes 18362368 | tf_op jit(solution)/shard_map/while/body/eval_jaxpr/vmap(tkgd,lkd->tkgl)/dot_general | solution.py:42
  437.1 7.6 %fusion.72 = f32[2,64,2,8,128]{4,1,3,0,2:T(8,128)S(1)} fusion(bf16[2048,2,128,1,1]{0,2,4,3,1:T(8,128)(2,1)S(1)} %bitcast.142, f32[2,2048,2,64,8]{1,3,4,2,0:T(8,128)} %get-tuple-element.168, f32[2,64,2,8]{1,3,0,2:T(8,128)S(1)} %get-tuple-element.169, pred[2,2048]{1,0:T(4,128)(4,1)S(1)} %compare_bitcast_fusion.2), kind=kOutput, calls=%fused_computation.12.clone.1 | convolution fusion | flops 1090519040 | bytes 18886656 | tf_op jit(solution)/shard_map/while/body/eval_jaxpr/vmap(tkgl,lkd->tkgd)/dot_general | solution.py:51
  444.6 7.8 %fusion.73 = f32[2,64,2,8]{1,3,0,2:T(8,128)S(1)} fusion(f32[2,2048,2,64,8]{1,3,4,2,0:T(8,128)} %get-tuple-element.168, f32[2,64,2,8]{1,3,0,2:T(8,128)S(1)} %get-tuple-element.169, pred[2,2048]{1,0:T(4,128)(4,1)S(1)} %compare_bitcast_fusion.2), kind=kLoop, calls=%fused_computation.7.clone.1 | loop fusion | flops 16775168 | bytes 16797696 | tf_op jit(solution)/shard_map/while/body/eval_jaxpr/vmap()/reduce_sum | solution.py:48
  460.1 7.1 %fusion.71 = (f32[2,64,2,8]{1,3,0,2:T(8,128)S(1)}, f32[2,2048,2,64,8]{1,3,4,2,0:T(8,128)}) fusion(pred[2,2048]{1,0:T(4,128)(4,1)S(1)} %compare_bitcast_fusion.2, bf16[2048,2,128,1,1]{0,2,4,3,1:T(8,128)(2,1)S(1)} %bitcast.138, bf16[2,64,2,8,128]{4,3,2,1,0:T(8,128)(2,1)S(1)} %dynamic-slice_bitcast_fusion.2), kind=kOutput, calls=%fused_computation.9.clone.1 | convolution fusion | flops 1086322688 | bytes 18362368 | tf_op jit(solution)/shard_map/while/body/eval_jaxpr/vmap(tkgd,lkd->tkgl)/dot_general | solution.py:42
  467.2 7.6 %fusion.72 = f32[2,64,2,8,128]{4,1,3,0,2:T(8,128)S(1)} fusion(bf16[2048,2,128,1,1]{0,2,4,3,1:T(8,128)(2,1)S(1)} %bitcast.142, f32[2,2048,2,64,8]{1,3,4,2,0:T(8,128)} %get-tuple-element.168, f32[2,64,2,8]{1,3,0,2:T(8,128)S(1)} %get-tuple-element.169, pred[2,2048]{1,0:T(4,128)(4,1)S(1)} %compare_bitcast_fusion.2), kind=kOutput, calls=%fused_computation.12.clone.1 | convolution fusion | flops 1090519040 | bytes 18886656 | tf_op jit(solution)/shard_map/while/body/eval_jaxpr/vmap(tkgl,lkd->tkgd)/dot_general | solution.py:51
  474.8 7.8 %fusion.73 = f32[2,64,2,8]{1,3,0,2:T(8,128)S(1)} fusion(f32[2,2048,2,64,8]{1,3,4,2,0:T(8,128)} %get-tuple-element.168, f32[2,64,2,8]{1,3,0,2:T(8,128)S(1)} %get-tuple-element.169, pred[2,2048]{1,0:T(4,128)(4,1)S(1)} %compare_bitcast_fusion.2), kind=kLoop, calls=%fused_computation.7.clone.1 | loop fusion | flops 16775168 | bytes 16797696 | tf_op jit(solution)/shard_map/while/body/eval_jaxpr/vmap()/reduce_sum | solution.py:48
  490.3 7.1 %fusion.71 = (f32[2,64,2,8]{1,3,0,2:T(8,128)S(1)}, f32[2,2048,2,64,8]{1,3,4,2,0:T(8,128)}) fusion(pred[2,2048]{1,0:T(4,128)(4,1)S(1)} %compare_bitcast_fusion.2, bf16[2048,2,128,1,1]{0,2,4,3,1:T(8,128)(2,1)S(1)} %bitcast.138, bf16[2,64,2,8,128]{4,3,2,1,0:T(8,128)(2,1)S(1)} %dynamic-slice_bitcast_fusion.2), kind=kOutput, calls=%fused_computation.9.clone.1 | convolution fusion | flops 1086322688 | bytes 18362368 | tf_op jit(solution)/shard_map/while/body/eval_jaxpr/vmap(tkgd,lkd->tkgl)/dot_general | solution.py:42
  497.4 7.6 %fusion.72 = f32[2,64,2,8,128]{4,1,3,0,2:T(8,128)S(1)} fusion(bf16[2048,2,128,1,1]{0,2,4,3,1:T(8,128)(2,1)S(1)} %bitcast.142, f32[2,2048,2,64,8]{1,3,4,2,0:T(8,128)} %get-tuple-element.168, f32[2,64,2,8]{1,3,0,2:T(8,128)S(1)} %get-tuple-element.169, pred[2,2048]{1,0:T(4,128)(4,1)S(1)} %compare_bitcast_fusion.2), kind=kOutput, calls=%fused_computation.12.clone.1 | convolution fusion | flops 1090519040 | bytes 18886656 | tf_op jit(solution)/shard_map/while/body/eval_jaxpr/vmap(tkgl,lkd->tkgd)/dot_general | solution.py:51
  505.0 7.8 %fusion.73 = f32[2,64,2,8]{1,3,0,2:T(8,128)S(1)} fusion(f32[2,2048,2,64,8]{1,3,4,2,0:T(8,128)} %get-tuple-element.168, f32[2,64,2,8]{1,3,0,2:T(8,128)S(1)} %get-tuple-element.169, pred[2,2048]{1,0:T(4,128)(4,1)S(1)} %compare_bitcast_fusion.2), kind=kLoop, calls=%fused_computation.7.clone.1 | loop fusion | flops 16775168 | bytes 16797696 | tf_op jit(solution)/shard_map/while/body/eval_jaxpr/vmap()/reduce_sum | solution.py:48
  520.4 7.1 %fusion.71 = (f32[2,64,2,8]{1,3,0,2:T(8,128)S(1)}, f32[2,2048,2,64,8]{1,3,4,2,0:T(8,128)}) fusion(pred[2,2048]{1,0:T(4,128)(4,1)S(1)} %compare_bitcast_fusion.2, bf16[2048,2,128,1,1]{0,2,4,3,1:T(8,128)(2,1)S(1)} %bitcast.138, bf16[2,64,2,8,128]{4,3,2,1,0:T(8,128)(2,1)S(1)} %dynamic-slice_bitcast_fusion.2), kind=kOutput, calls=%fused_computation.9.clone.1 | convolution fusion | flops 1086322688 | bytes 18362368 | tf_op jit(solution)/shard_map/while/body/eval_jaxpr/vmap(tkgd,lkd->tkgl)/dot_general | solution.py:42
  527.6 7.6 %fusion.72 = f32[2,64,2,8,128]{4,1,3,0,2:T(8,128)S(1)} fusion(bf16[2048,2,128,1,1]{0,2,4,3,1:T(8,128)(2,1)S(1)} %bitcast.142, f32[2,2048,2,64,8]{1,3,4,2,0:T(8,128)} %get-tuple-element.168, f32[2,64,2,8]{1,3,0,2:T(8,128)S(1)} %get-tuple-element.169, pred[2,2048]{1,0:T(4,128)(4,1)S(1)} %compare_bitcast_fusion.2), kind=kOutput, calls=%fused_computation.12.clone.1 | convolution fusion | flops 1090519040 | bytes 18886656 | tf_op jit(solution)/shard_map/while/body/eval_jaxpr/vmap(tkgl,lkd->tkgd)/dot_general | solution.py:51
  535.1 7.8 %fusion.73 = f32[2,64,2,8]{1,3,0,2:T(8,128)S(1)} fusion(f32[2,2048,2,64,8]{1,3,4,2,0:T(8,128)} %get-tuple-element.168, f32[2,64,2,8]{1,3,0,2:T(8,128)S(1)} %get-tuple-element.169, pred[2,2048]{1,0:T(4,128)(4,1)S(1)} %compare_bitcast_fusion.2), kind=kLoop, calls=%fused_computation.7.clone.1 | loop fusion | flops 16775168 | bytes 16797696 | tf_op jit(solution)/shard_map/while/body/eval_jaxpr/vmap()/reduce_sum | solution.py:48
  550.6 7.1 %fusion.71 = (f32[2,64,2,8]{1,3,0,2:T(8,128)S(1)}, f32[2,2048,2,64,8]{1,3,4,2,0:T(8,128)}) fusion(pred[2,2048]{1,0:T(4,128)(4,1)S(1)} %compare_bitcast_fusion.2, bf16[2048,2,128,1,1]{0,2,4,3,1:T(8,128)(2,1)S(1)} %bitcast.138, bf16[2,64,2,8,128]{4,3,2,1,0:T(8,128)(2,1)S(1)} %dynamic-slice_bitcast_fusion.2), kind=kOutput, calls=%fused_computation.9.clone.1 | convolution fusion | flops 1086322688 | bytes 18362368 | tf_op jit(solution)/shard_map/while/body/eval_jaxpr/vmap(tkgd,lkd->tkgl)/dot_general | solution.py:42
  557.7 7.6 %fusion.72 = f32[2,64,2,8,128]{4,1,3,0,2:T(8,128)S(1)} fusion(bf16[2048,2,128,1,1]{0,2,4,3,1:T(8,128)(2,1)S(1)} %bitcast.142, f32[2,2048,2,64,8]{1,3,4,2,0:T(8,128)} %get-tuple-element.168, f32[2,64,2,8]{1,3,0,2:T(8,128)S(1)} %get-tuple-element.169, pred[2,2048]{1,0:T(4,128)(4,1)S(1)} %compare_bitcast_fusion.2), kind=kOutput, calls=%fused_computation.12.clone.1 | convolution fusion | flops 1090519040 | bytes 18886656 | tf_op jit(solution)/shard_map/while/body/eval_jaxpr/vmap(tkgl,lkd->tkgd)/dot_general | solution.py:51
  565.3 7.8 %fusion.73 = f32[2,64,2,8]{1,3,0,2:T(8,128)S(1)} fusion(f32[2,2048,2,64,8]{1,3,4,2,0:T(8,128)} %get-tuple-element.168, f32[2,64,2,8]{1,3,0,2:T(8,128)S(1)} %get-tuple-element.169, pred[2,2048]{1,0:T(4,128)(4,1)S(1)} %compare_bitcast_fusion.2), kind=kLoop, calls=%fused_computation.7.clone.1 | loop fusion | flops 16775168 | bytes 16797696 | tf_op jit(solution)/shard_map/while/body/eval_jaxpr/vmap()/reduce_sum | solution.py:48
  580.8 7.1 %fusion.71 = (f32[2,64,2,8]{1,3,0,2:T(8,128)S(1)}, f32[2,2048,2,64,8]{1,3,4,2,0:T(8,128)}) fusion(pred[2,2048]{1,0:T(4,128)(4,1)S(1)} %compare_bitcast_fusion.2, bf16[2048,2,128,1,1]{0,2,4,3,1:T(8,128)(2,1)S(1)} %bitcast.138, bf16[2,64,2,8,128]{4,3,2,1,0:T(8,128)(2,1)S(1)} %dynamic-slice_bitcast_fusion.2), kind=kOutput, calls=%fused_computation.9.clone.1 | convolution fusion | flops 1086322688 | bytes 18362368 | tf_op jit(solution)/shard_map/while/body/eval_jaxpr/vmap(tkgd,lkd->tkgl)/dot_general | solution.py:42
  587.9 7.6 %fusion.72 = f32[2,64,2,8,128]{4,1,3,0,2:T(8,128)S(1)} fusion(bf16[2048,2,128,1,1]{0,2,4,3,1:T(8,128)(2,1)S(1)} %bitcast.142, f32[2,2048,2,64,8]{1,3,4,2,0:T(8,128)} %get-tuple-element.168, f32[2,64,2,8]{1,3,0,2:T(8,128)S(1)} %get-tuple-element.169, pred[2,2048]{1,0:T(4,128)(4,1)S(1)} %compare_bitcast_fusion.2), kind=kOutput, calls=%fused_computation.12.clone.1 | convolution fusion | flops 1090519040 | bytes 18886656 | tf_op jit(solution)/shard_map/while/body/eval_jaxpr/vmap(tkgl,lkd->tkgd)/dot_general | solution.py:51
  595.5 7.8 %fusion.73 = f32[2,64,2,8]{1,3,0,2:T(8,128)S(1)} fusion(f32[2,2048,2,64,8]{1,3,4,2,0:T(8,128)} %get-tuple-element.168, f32[2,64,2,8]{1,3,0,2:T(8,128)S(1)} %get-tuple-element.169, pred[2,2048]{1,0:T(4,128)(4,1)S(1)} %compare_bitcast_fusion.2), kind=kLoop, calls=%fused_computation.7.clone.1 | loop fusion | flops 16775168 | bytes 16797696 | tf_op jit(solution)/shard_map/while/body/eval_jaxpr/vmap()/reduce_sum | solution.py:48
  611.0 7.1 %fusion.71 = (f32[2,64,2,8]{1,3,0,2:T(8,128)S(1)}, f32[2,2048,2,64,8]{1,3,4,2,0:T(8,128)}) fusion(pred[2,2048]{1,0:T(4,128)(4,1)S(1)} %compare_bitcast_fusion.2, bf16[2048,2,128,1,1]{0,2,4,3,1:T(8,128)(2,1)S(1)} %bitcast.138, bf16[2,64,2,8,128]{4,3,2,1,0:T(8,128)(2,1)S(1)} %dynamic-slice_bitcast_fusion.2), kind=kOutput, calls=%fused_computation.9.clone.1 | convolution fusion | flops 1086322688 | bytes 18362368 | tf_op jit(solution)/shard_map/while/body/eval_jaxpr/vmap(tkgd,lkd->tkgl)/dot_general | solution.py:42
  618.1 7.6 %fusion.72 = f32[2,64,2,8,128]{4,1,3,0,2:T(8,128)S(1)} fusion(bf16[2048,2,128,1,1]{0,2,4,3,1:T(8,128)(2,1)S(1)} %bitcast.142, f32[2,2048,2,64,8]{1,3,4,2,0:T(8,128)} %get-tuple-element.168, f32[2,64,2,8]{1,3,0,2:T(8,128)S(1)} %get-tuple-element.169, pred[2,2048]{1,0:T(4,128)(4,1)S(1)} %compare_bitcast_fusion.2), kind=kOutput, calls=%fused_computation.12.clone.1 | convolution fusion | flops 1090519040 | bytes 18886656 | tf_op jit(solution)/shard_map/while/body/eval_jaxpr/vmap(tkgl,lkd->tkgd)/dot_general | solution.py:51
  625.7 7.8 %fusion.73 = f32[2,64,2,8]{1,3,0,2:T(8,128)S(1)} fusion(f32[2,2048,2,64,8]{1,3,4,2,0:T(8,128)} %get-tuple-element.168, f32[2,64,2,8]{1,3,0,2:T(8,128)S(1)} %get-tuple-element.169, pred[2,2048]{1,0:T(4,128)(4,1)S(1)} %compare_bitcast_fusion.2), kind=kLoop, calls=%fused_computation.7.clone.1 | loop fusion | flops 16775168 | bytes 16797696 | tf_op jit(solution)/shard_map/while/body/eval_jaxpr/vmap()/reduce_sum | solution.py:48
  641.1 7.1 %fusion.71 = (f32[2,64,2,8]{1,3,0,2:T(8,128)S(1)}, f32[2,2048,2,64,8]{1,3,4,2,0:T(8,128)}) fusion(pred[2,2048]{1,0:T(4,128)(4,1)S(1)} %compare_bitcast_fusion.2, bf16[2048,2,128,1,1]{0,2,4,3,1:T(8,128)(2,1)S(1)} %bitcast.138, bf16[2,64,2,8,128]{4,3,2,1,0:T(8,128)(2,1)S(1)} %dynamic-slice_bitcast_fusion.2), kind=kOutput, calls=%fused_computation.9.clone.1 | convolution fusion | flops 1086322688 | bytes 18362368 | tf_op jit(solution)/shard_map/while/body/eval_jaxpr/vmap(tkgd,lkd->tkgl)/dot_general | solution.py:42
  648.2 7.6 %fusion.72 = f32[2,64,2,8,128]{4,1,3,0,2:T(8,128)S(1)} fusion(bf16[2048,2,128,1,1]{0,2,4,3,1:T(8,128)(2,1)S(1)} %bitcast.142, f32[2,2048,2,64,8]{1,3,4,2,0:T(8,128)} %get-tuple-element.168, f32[2,64,2,8]{1,3,0,2:T(8,128)S(1)} %get-tuple-element.169, pred[2,2048]{1,0:T(4,128)(4,1)S(1)} %compare_bitcast_fusion.2), kind=kOutput, calls=%fused_computation.12.clone.1 | convolution fusion | flops 1090519040 | bytes 18886656 | tf_op jit(solution)/shard_map/while/body/eval_jaxpr/vmap(tkgl,lkd->tkgd)/dot_general | solution.py:51
  655.8 7.8 %fusion.73 = f32[2,64,2,8]{1,3,0,2:T(8,128)S(1)} fusion(f32[2,2048,2,64,8]{1,3,4,2,0:T(8,128)} %get-tuple-element.168, f32[2,64,2,8]{1,3,0,2:T(8,128)S(1)} %get-tuple-element.169, pred[2,2048]{1,0:T(4,128)(4,1)S(1)} %compare_bitcast_fusion.2), kind=kLoop, calls=%fused_computation.7.clone.1 | loop fusion | flops 16775168 | bytes 16797696 | tf_op jit(solution)/shard_map/while/body/eval_jaxpr/vmap()/reduce_sum | solution.py:48
  (207 shorter events, 113.2 us)
Async XLA Ops:
  6.5 40.7 %all-gather.11.cloned.1.call-start = ((), (), s32[]{:S(2)}) async-start(), calls=%async_computation.2 | async-start | bytes 2621440 | tf_op jit(solution)/shard_map/all_gather | solution.py:97
  7.3 70.7 %all-gather.15.cloned.1.call-start = ((), (), s32[]{:S(2)}) async-start(), calls=%async_computation.4 | async-start | bytes 2359296 | tf_op jit(solution)/shard_map/all_gather | solution.py:106
  8.0 100.2 %all-gather.17.cloned.1.call-start = ((), (), s32[]{:S(2)}) async-start(), calls=%async_computation.5 | async-start | bytes 2359296 | tf_op jit(solution)/shard_map/all_gather | solution.py:111
  8.7 1.8 copy-start.16
  8.8 4.3 copy-start
  8.8 251.5 %all-gather.13.cloned.1.call-start = ((), (), s32[]{:S(2)}) async-start(), calls=%async_computation.3 | async-start | bytes 18874368 | tf_op jit(solution)/shard_map/all_gather | solution.py:101
  9.3 332.7 %all-gather.9.cloned.1.call-start = ((), (), s32[]{:S(2)}) async-start(), calls=%async_computation.1 | async-start | bytes 9437184 | tf_op jit(solution)/shard_map/all_gather | solution.py:156
  9.9 68.1 %copy-start.17 = (f32[4096]{0:T(1024)S(1)}, f32[4096]{0:T(1024)}, u32[]{:S(2)}) copy-start(f32[4096]{0:T(1024)} %param.17) | copy-start | bytes 49156
  9.9 68.1 %copy-start.19 = (f32[256]{0:T(256)S(1)}, f32[256]{0:T(256)}, u32[]{:S(2)}) copy-start(f32[256]{0:T(256)} %param.22) | copy-start | bytes 3076
  9.9 414.2 %all-gather.7.cloned.1.call-start = ((), (), s32[]{:S(2)}) async-start(), calls=%async_computation | async-start | bytes 9437184 | tf_op jit(solution)/shard_map/all_gather | solution.py:157
  12.2 3.2 copy-start.14
  47.3 30.7 %copy-start.7 = (bf16[256,4096]{1,0:T(8,128)(2,1)S(1)}, bf16[256,4096]{1,0:T(8,128)(2,1)}, u32[]{:S(2)}) copy-start(bf16[256,4096]{1,0:T(8,128)(2,1)} %all-gather.11.cloned.1.call-done) | copy-start | bytes 6291460
  49.5 58.7 %copy-start.20 = (f32[256]{0:T(256)S(1)}, f32[256]{0:T(256)}, u32[]{:S(2)}) copy-start(f32[256]{0:T(256)} %param.23) | copy-start | bytes 3076
  80.5 179.8 %copy-start.18 = (f32[2048]{0:T(1024)S(1)}, f32[2048]{0:T(1024)}, u32[]{:S(2)}) copy-start(f32[2048]{0:T(1024)} %param.21) | copy-start | bytes 24580
  269.6 2.0 copy-start.5
  273.9 1.4 copy-start.2
  283.5 3.0 copy-start.3
  287.0 137.1 %copy-start.8 = (f32[8,2,64,16]{2,3,1,0:T(8,128)S(1)}, f32[8,2,64,16]{2,3,1,0:T(8,128)}, u32[]{:S(2)}) copy-start(f32[8,2,64,16]{2,3,1,0:T(8,128)} %custom-call.12) | copy-start | bytes 196612
  287.0 137.1 %copy-start.9 = (f32[8,2,64,16]{2,3,1,0:T(8,128)S(1)}, f32[8,2,64,16]{2,3,1,0:T(8,128)}, u32[]{:S(2)}) copy-start(f32[8,2,64,16]{2,3,1,0:T(8,128)} %custom-call.11) | copy-start | bytes 196612
  429.9 7.1 %copy-start.1 = (bf16[1,2048,256]{1,2,0:T(8,128)(2,1)S(1)}, bf16[1,2048,256]{1,2,0:T(8,128)(2,1)}, u32[]{:S(2)}) copy-start(bf16[1,2048,256]{1,2,0:T(8,128)(2,1)} %copy.160) | copy-start | bytes 3145732 | tf_op jit(solution)/shard_map/while
  460.1 7.1 %copy-start.1 = (bf16[1,2048,256]{1,2,0:T(8,128)(2,1)S(1)}, bf16[1,2048,256]{1,2,0:T(8,128)(2,1)}, u32[]{:S(2)}) copy-start(bf16[1,2048,256]{1,2,0:T(8,128)(2,1)} %copy.160) | copy-start | bytes 3145732 | tf_op jit(solution)/shard_map/while
  490.3 7.1 %copy-start.1 = (bf16[1,2048,256]{1,2,0:T(8,128)(2,1)S(1)}, bf16[1,2048,256]{1,2,0:T(8,128)(2,1)}, u32[]{:S(2)}) copy-start(bf16[1,2048,256]{1,2,0:T(8,128)(2,1)} %copy.160) | copy-start | bytes 3145732 | tf_op jit(solution)/shard_map/while
  520.4 7.1 %copy-start.1 = (bf16[1,2048,256]{1,2,0:T(8,128)(2,1)S(1)}, bf16[1,2048,256]{1,2,0:T(8,128)(2,1)}, u32[]{:S(2)}) copy-start(bf16[1,2048,256]{1,2,0:T(8,128)(2,1)} %copy.160) | copy-start | bytes 3145732 | tf_op jit(solution)/shard_map/while
  550.6 7.1 %copy-start.1 = (bf16[1,2048,256]{1,2,0:T(8,128)(2,1)S(1)}, bf16[1,2048,256]{1,2,0:T(8,128)(2,1)}, u32[]{:S(2)}) copy-start(bf16[1,2048,256]{1,2,0:T(8,128)(2,1)} %copy.160) | copy-start | bytes 3145732 | tf_op jit(solution)/shard_map/while
  580.8 7.1 %copy-start.1 = (bf16[1,2048,256]{1,2,0:T(8,128)(2,1)S(1)}, bf16[1,2048,256]{1,2,0:T(8,128)(2,1)}, u32[]{:S(2)}) copy-start(bf16[1,2048,256]{1,2,0:T(8,128)(2,1)} %copy.160) | copy-start | bytes 3145732 | tf_op jit(solution)/shard_map/while
  611.0 7.1 %copy-start.1 = (bf16[1,2048,256]{1,2,0:T(8,128)(2,1)S(1)}, bf16[1,2048,256]{1,2,0:T(8,128)(2,1)}, u32[]{:S(2)}) copy-start(bf16[1,2048,256]{1,2,0:T(8,128)(2,1)} %copy.160) | copy-start | bytes 3145732 | tf_op jit(solution)/shard_map/while
  641.1 7.1 %copy-start.1 = (bf16[1,2048,256]{1,2,0:T(8,128)(2,1)S(1)}, bf16[1,2048,256]{1,2,0:T(8,128)(2,1)}, u32[]{:S(2)}) copy-start(bf16[1,2048,256]{1,2,0:T(8,128)(2,1)} %copy.160) | copy-start | bytes 3145732 | tf_op jit(solution)/shard_map/while
  666.2 4.9 copy-start.11
  666.2 4.9 copy-start.15
  672.9 1.6 copy-start.6
  672.9 1.6 copy-start.12
  672.9 1.6 copy-start.13
  (2 other events, 1.8 us)
Sparse Core Ops, SparseCore 0:
  9.2 38.0 all-gather.10
  48.8 29.0 all-gather.14
  79.6 28.5 all-gather.16
  109.7 150.5 all-gather.12
  261.7 80.2 all-gather.8
  343.5 80.5 all-gather.6
where the time goes:
time: 687 us; the launch traced here: 686 us
  waiting for transfers between devices  374 us (54%)
  matrix products  133 us (19%)
  local copies, waits for them, and re-layouts  84.7 us (12%)
  other arithmetic  80.2 us (12%)
  between operations  13.9 us (2%)
    all_gather x1, waiting for transfers between devices, shards(): lax.all_gather(w_query, 'fsdp', axis=0, tiled=True)  150 us
    all_gather x1, waiting for transfers between devices, shards(): value_piece = lax.all_gather(value_cache, 'fsdp', axis=0, tiled=True)  82.1 us
    reduce_sum x9, other arithmetic, partial_attend(): total = jnp.sum(weights, axis=-1)  63 us
    dot_general x9, matrix products, partial_attend(): jnp.einsum('tkgl,lkd->tkgd', rounded, value_rows, preferred_element_type=...  61.1 us
    dot_general x9, matrix products, partial_attend(): jnp.einsum('tkgd,lkd->tkgl', grouped, key_rows, preferred_element_type=jn...  58.6 us
    all_gather x1, waiting for transfers between devices, shards(): key_piece = lax.all_gather(key_cache, 'fsdp', axis=0, tiled=True)  50.4 us
    dynamic_slice x32, local copies, waits for them, and re-layouts, shards(): lax.map(one_document, (slot_queries.reshape((count, CAP) + slot_queries.s...  37.3 us
    all_gather x1, waiting for transfers between devices, shards(): full_rows = lax.all_gather(inputs, 'corpus', axis=1, tiled=True)  31.9 us
  transfers between devices with their start and end apart: 6, of which 6 were waited for; matrix products, arithmetic and copies ran while one was open for 6% of the time, Pallas kernels for 0%

commit v1 on v0

--- a/solution.py
+++ b/solution.py
@@ -2,6 +2,7 @@
 import jax.numpy as jnp
 from jax import lax
 from jax.sharding import PartitionSpec as P
+from jax.lax import axis_index, axis_size, ppermute
 
 HD = 128
 SL = 64
@@ -9,6 +10,30 @@
 EPS = 1e-06
 THETA = 1000000.0
 MASKED = -1e30
+
+
+def bring_ports_in(m, k_dim):
+    big = list(m.shape[1:])
+    big[k_dim] *= m.shape[0]
+    return jnp.moveaxis(m, 0, k_dim).reshape(big)
+
+
+def edit_squares_here(piece_in, mesh_dim):
+    x_now = axis_size(mesh_dim)
+    y2 = axis_index(mesh_dim)
+    z2, x_new = (x_now, y2)
+    far_arr, block_next = (piece_in[None], 1)
+    while block_next < z2:
+        blocks_here = []
+        for i0 in [*range(z2)]:
+            blocks_here.append((i0, i0 ^ block_next))
+        everything = ppermute(far_arr, mesh_dim, perm=blocks_here)
+        kept_arr = x_new & block_next == 0
+        far_arr = jnp.concatenate(
+            [jnp.where(kept_arr, far_arr, everything), jnp.where(kept_arr, everything, far_arr)]
+        )
+        block_next *= 2
+    return far_arr
 
 
 def rope_tables(position, width):
@@ -94,7 +119,7 @@
     source_doc,
     prefix_len,
 ):
-    full_rows = lax.all_gather(inputs, "corpus", axis=1, tiled=True)
+    full_rows = bring_ports_in(edit_squares_here(inputs, "corpus"), 1)
     normed = normalize(full_rows, norm_gain)
     query_lin = jnp.dot(
         normed,

time: 687 us -> 650 us (0.946)
  waiting for transfers between devices: 374 us -> 331 us
    all_gather x1 -> x0, waiting for transfers between devices: 31.9 us -> none  [shards(): full_rows = lax.all_gather(inputs, 'corpus', axis=1, tiled=True)]
    ppermute x0 -> x2, waiting for transfers between devices: none -> 30.6 us  [edit_squares_here(): everything = ppermute(far_arr, mesh_dim, perm=blocks_here)]
    all_gather x1, waiting for transfers between devices: 28.5 us -> 0.02 us  [shards(): lax.all_gather(w_key, 'fsdp', axis=0, tiled=True)]
    all_gather x1, waiting for transfers between devices: 27.7 us -> 15.1 us  [shards(): lax.all_gather(w_value, 'fsdp', axis=0, tiled=True)]
  transfers between devices with their start and end apart: 6 -> 7, of which waited for: 6 -> 6; matrix products, arithmetic and copies ran while one was open for 6% -> 6% of each run, Pallas kernels for 0% -> 0%
where the time goes in v1:
time: 650 us; the launch traced here: 648 us
  waiting for transfers between devices  331 us (51%)
  matrix products  133 us (20%)
  local copies, waits for them, and re-layouts  84.8 us (13%)
  other arithmetic  81 us (12%)
  between operations  13.6 us (2%)
    all_gather x1, waiting for transfers between devices, shards(): lax.all_gather(w_query, 'fsdp', axis=0, tiled=True)  150 us
    all_gather x1, waiting for transfers between devices, shards(): value_piece = lax.all_gather(value_cache, 'fsdp', axis=0, tiled=True)  82.1 us
    reduce_sum x9, other arithmetic, partial_attend(): total = jnp.sum(weights, axis=-1)  63 us
    dot_general x9, matrix products, partial_attend(): jnp.einsum('tkgl,lkd->tkgd', rounded, value_rows, preferred_element_type=...  61.1 us
    dot_general x9, matrix products, partial_attend(): jnp.einsum('tkgd,lkd->tkgl', grouped, key_rows, preferred_element_type=jn...  58.6 us
    all_gather x1, waiting for transfers between devices, shards(): key_piece = lax.all_gather(key_cache, 'fsdp', axis=0, tiled=True)  50.3 us
    dynamic_slice x32, local copies, waits for them, and re-layouts, shards(): lax.map(one_document, (slot_queries.reshape((count, CAP) + slot_queries.s...  37.3 us
    ppermute x2, waiting for transfers between devices, edit_squares_here(): everything = ppermute(far_arr, mesh_dim, perm=blocks_here)  30.6 us
  transfers between devices with their start and end apart: 7, of which 6 were waited for; matrix products, arithmetic and copies ran while one was open for 6% of the time, Pallas kernels for 0%

profile of v1, /device:TPU:0, one launch (start us, length us, event | category | flops | bytes accessed | tf_op | source)
XLA Modules:
  0.0 648.3 jit_solution(15689747005448410619)
XLA Ops:
  14.3 10.8 %collective-permute-done = bf16[1,256,1024]{1,2,0:T(8,128)(2,1)S(1)} collective-permute-done((bf16[1,256,1024]{1,2,0:T(8,128)(2,1)S(1)}, bf16[1,256,1024]{1,2,0:T(8,128)(2,1)S(1)}, u32[]{:S(2)}, u32[]{:S(2)}) %collective-permute-start) | collective-permute-done | bytes 524320 | tf_op jit(solution)/shard_map/ppermute | solution.py:30
  31.1 19.7 %collective-permute-done.1 = bf16[2,256,1024]{1,2,0:T(8,128)(2,1)S(1)} collective-permute-done((bf16[2,256,1024]{1,2,0:T(8,128)(2,1)}, bf16[2,256,1024]{1,2,0:T(8,128)(2,1)S(1)}, u32[]{:S(2)}, u32[]{:S(2)}) %collective-permute-start.1) | collective-permute-done | bytes 1048608 | tf_op jit(solution)/shard_map/ppermute | solution.py:30
  55.9 15.1 %all-gather.14.cloned.1.call-done = bf16[4096,256]{1,0:T(8,128)(2,1)} async-done(((bf16[512,256]{1,0:T(8,128)(2,1)}), bf16[4096,256]{1,0:T(8,128)(2,1)}) %all-gather.14.cloned.1.call-update) | async-done | bytes 2097168 | tf_op jit(solution)/shard_map/all_gather | solution.py:136
  73.6 149.7 %all-gather.10.cloned.1.call-done = bf16[4096,2048]{1,0:T(8,128)(2,1)} async-done(((bf16[512,2048]{1,0:T(8,128)(2,1)}), bf16[4096,2048]{1,0:T(8,128)(2,1)}) %all-gather.10.cloned.1.call-update) | async-done | bytes 16777232 | tf_op jit(solution)/shard_map/all_gather | solution.py:126
  223.3 8.1 %fusion.25 = f32[32,8,16,128]{3,1,2,0:T(8,128)S(1)} fusion(bf16[256,4096]{0,1:T(8,128)(2,1)S(1)} %fusion.14, bf16[4096,2048]{1,0:T(8,128)(2,1)} %all-gather.10.cloned.1.call-done, f32[2048]{0:T(1024)S(1)} %copy-done.11), kind=kOutput, calls=%fused_computation.52 | convolution fusion | flops 4295491584 | bytes 20979712 | tf_op jit(solution)/shard_map/dot_general | solution.py:124
  254.7 50.3 %all-gather.8.cloned.1.call-done = bf16[8,2048,256]{2,1,0:T(8,128)(2,1)} async-done(((bf16[1,2048,256]{2,1,0:T(8,128)(2,1)}), bf16[8,2048,256]{2,1,0:T(8,128)(2,1)}) %all-gather.8.cloned.1.call-update) | async-done | bytes 8388624 | tf_op jit(solution)/shard_map/all_gather | solution.py:181
  305.0 82.1 %all-gather.6.cloned.1.call-done = bf16[8,2048,256]{2,1,0:T(8,128)(2,1)} async-done(((bf16[1,2048,256]{2,1,0:T(8,128)(2,1)}), bf16[8,2048,256]{2,1,0:T(8,128)(2,1)}) %all-gather.6.cloned.1.call-update) | async-done | bytes 8388624 | tf_op jit(solution)/shard_map/all_gather | solution.py:182
  387.1 241.3 %while.14 = (s32[]{:T(128)}, f32[8,2,64,2048]{3,2,1,0:T(8,128)}, f32[8,2,64,16]{2,3,1,0:T(8,128)S(1)}, f32[8,2,64,16]{2,3,1,0:T(8,128)S(1)}, bf16[8,2048,256]{2,...) while((s32[]{:T(128)}, f32[8,2,64,2048]{3,2,1,0:T(8,128)}, ...), condition=%wide.region_7.8_spmd, body=%wide.region_4.7_spmd.sunk | while | flops 2193620992 | bytes 74047632 | solution.py:192
  392.9 7.1 %fusion.70 = (f32[2,64,2,8]{1,3,0,2:T(8,128)S(1)}, f32[2,2048,2,64,8]{1,3,4,2,0:T(8,128)}) fusion(pred[2,2048]{1,0:T(4,128)(4,1)S(1)} %compare_bitcast_fusion.2, bf16[2048,2,128,1,1]{0,2,4,3,1:T(8,128)(2,1)S(1)} %bitcast.152, bf16[2,64,2,8,128]{4,3,2,1,0:T(8,128)(2,1)S(1)} %dynamic-slice_bitcast_fusion.2), kind=kOutput, calls=%fused_computation.9.clone.1 | convolution fusion | flops 1086322688 | bytes 18362368 | tf_op jit(solution)/shard_map/while/body/eval_jaxpr/vmap(tkgd,lkd->tkgl)/dot_general | solution.py:67
  400.0 7.6 %fusion.71 = f32[2,64,2,8,128]{4,1,3,0,2:T(8,128)S(1)} fusion(bf16[2048,2,128,1,1]{0,2,4,3,1:T(8,128)(2,1)S(1)} %bitcast.156, f32[2,2048,2,64,8]{1,3,4,2,0:T(8,128)} %get-tuple-element.172, f32[2,64,2,8]{1,3,0,2:T(8,128)S(1)} %get-tuple-element.173, pred[2,2048]{1,0:T(4,128)(4,1)S(1)} %compare_bitcast_fusion.2), kind=kOutput, calls=%fused_computation.12.clone.1 | convolution fusion | flops 1090519040 | bytes 18886656 | tf_op jit(solution)/shard_map/while/body/eval_jaxpr/vmap(tkgl,lkd->tkgd)/dot_general | solution.py:76
  407.6 7.8 %fusion.72 = f32[2,64,2,8]{1,3,0,2:T(8,128)S(1)} fusion(f32[2,2048,2,64,8]{1,3,4,2,0:T(8,128)} %get-tuple-element.172, f32[2,64,2,8]{1,3,0,2:T(8,128)S(1)} %get-tuple-element.173, pred[2,2048]{1,0:T(4,128)(4,1)S(1)} %compare_bitcast_fusion.2), kind=kLoop, calls=%fused_computation.7.clone.1 | loop fusion | flops 16775168 | bytes 16797696 | tf_op jit(solution)/shard_map/while/body/eval_jaxpr/vmap()/reduce_sum | solution.py:73
  423.1 7.1 %fusion.70 = (f32[2,64,2,8]{1,3,0,2:T(8,128)S(1)}, f32[2,2048,2,64,8]{1,3,4,2,0:T(8,128)}) fusion(pred[2,2048]{1,0:T(4,128)(4,1)S(1)} %compare_bitcast_fusion.2, bf16[2048,2,128,1,1]{0,2,4,3,1:T(8,128)(2,1)S(1)} %bitcast.152, bf16[2,64,2,8,128]{4,3,2,1,0:T(8,128)(2,1)S(1)} %dynamic-slice_bitcast_fusion.2), kind=kOutput, calls=%fused_computation.9.clone.1 | convolution fusion | flops 1086322688 | bytes 18362368 | tf_op jit(solution)/shard_map/while/body/eval_jaxpr/vmap(tkgd,lkd->tkgl)/dot_general | solution.py:67
  430.2 7.6 %fusion.71 = f32[2,64,2,8,128]{4,1,3,0,2:T(8,128)S(1)} fusion(bf16[2048,2,128,1,1]{0,2,4,3,1:T(8,128)(2,1)S(1)} %bitcast.156, f32[2,2048,2,64,8]{1,3,4,2,0:T(8,128)} %get-tuple-element.172, f32[2,64,2,8]{1,3,0,2:T(8,128)S(1)} %get-tuple-element.173, pred[2,2048]{1,0:T(4,128)(4,1)S(1)} %compare_bitcast_fusion.2), kind=kOutput, calls=%fused_computation.12.clone.1 | convolution fusion | flops 1090519040 | bytes 18886656 | tf_op jit(solution)/shard_map/while/body/eval_jaxpr/vmap(tkgl,lkd->tkgd)/dot_general | solution.py:76
  437.8 7.8 %fusion.72 = f32[2,64,2,8]{1,3,0,2:T(8,128)S(1)} fusion(f32[2,2048,2,64,8]{1,3,4,2,0:T(8,128)} %get-tuple-element.172, f32[2,64,2,8]{1,3,0,2:T(8,128)S(1)} %get-tuple-element.173, pred[2,2048]{1,0:T(4,128)(4,1)S(1)} %compare_bitcast_fusion.2), kind=kLoop, calls=%fused_computation.7.clone.1 | loop fusion | flops 16775168 | bytes 16797696 | tf_op jit(solution)/shard_map/while/body/eval_jaxpr/vmap()/reduce_sum | solution.py:73
  453.2 7.1 %fusion.70 = (f32[2,64,2,8]{1,3,0,2:T(8,128)S(1)}, f32[2,2048,2,64,8]{1,3,4,2,0:T(8,128)}) fusion(pred[2,2048]{1,0:T(4,128)(4,1)S(1)} %compare_bitcast_fusion.2, bf16[2048,2,128,1,1]{0,2,4,3,1:T(8,128)(2,1)S(1)} %bitcast.152, bf16[2,64,2,8,128]{4,3,2,1,0:T(8,128)(2,1)S(1)} %dynamic-slice_bitcast_fusion.2), kind=kOutput, calls=%fused_computation.9.clone.1 | convolution fusion | flops 1086322688 | bytes 18362368 | tf_op jit(solution)/shard_map/while/body/eval_jaxpr/vmap(tkgd,lkd->tkgl)/dot_general | solution.py:67
  460.3 7.6 %fusion.71 = f32[2,64,2,8,128]{4,1,3,0,2:T(8,128)S(1)} fusion(bf16[2048,2,128,1,1]{0,2,4,3,1:T(8,128)(2,1)S(1)} %bitcast.156, f32[2,2048,2,64,8]{1,3,4,2,0:T(8,128)} %get-tuple-element.172, f32[2,64,2,8]{1,3,0,2:T(8,128)S(1)} %get-tuple-element.173, pred[2,2048]{1,0:T(4,128)(4,1)S(1)} %compare_bitcast_fusion.2), kind=kOutput, calls=%fused_computation.12.clone.1 | convolution fusion | flops 1090519040 | bytes 18886656 | tf_op jit(solution)/shard_map/while/body/eval_jaxpr/vmap(tkgl,lkd->tkgd)/dot_general | solution.py:76
  467.9 7.8 %fusion.72 = f32[2,64,2,8]{1,3,0,2:T(8,128)S(1)} fusion(f32[2,2048,2,64,8]{1,3,4,2,0:T(8,128)} %get-tuple-element.172, f32[2,64,2,8]{1,3,0,2:T(8,128)S(1)} %get-tuple-element.173, pred[2,2048]{1,0:T(4,128)(4,1)S(1)} %compare_bitcast_fusion.2), kind=kLoop, calls=%fused_computation.7.clone.1 | loop fusion | flops 16775168 | bytes 16797696 | tf_op jit(solution)/shard_map/while/body/eval_jaxpr/vmap()/reduce_sum | solution.py:73
  483.4 7.1 %fusion.70 = (f32[2,64,2,8]{1,3,0,2:T(8,128)S(1)}, f32[2,2048,2,64,8]{1,3,4,2,0:T(8,128)}) fusion(pred[2,2048]{1,0:T(4,128)(4,1)S(1)} %compare_bitcast_fusion.2, bf16[2048,2,128,1,1]{0,2,4,3,1:T(8,128)(2,1)S(1)} %bitcast.152, bf16[2,64,2,8,128]{4,3,2,1,0:T(8,128)(2,1)S(1)} %dynamic-slice_bitcast_fusion.2), kind=kOutput, calls=%fused_computation.9.clone.1 | convolution fusion | flops 1086322688 | bytes 18362368 | tf_op jit(solution)/shard_map/while/body/eval_jaxpr/vmap(tkgd,lkd->tkgl)/dot_general | solution.py:67
  490.5 7.6 %fusion.71 = f32[2,64,2,8,128]{4,1,3,0,2:T(8,128)S(1)} fusion(bf16[2048,2,128,1,1]{0,2,4,3,1:T(8,128)(2,1)S(1)} %bitcast.156, f32[2,2048,2,64,8]{1,3,4,2,0:T(8,128)} %get-tuple-element.172, f32[2,64,2,8]{1,3,0,2:T(8,128)S(1)} %get-tuple-element.173, pred[2,2048]{1,0:T(4,128)(4,1)S(1)} %compare_bitcast_fusion.2), kind=kOutput, calls=%fused_computation.12.clone.1 | convolution fusion | flops 1090519040 | bytes 18886656 | tf_op jit(solution)/shard_map/while/body/eval_jaxpr/vmap(tkgl,lkd->tkgd)/dot_general | solution.py:76
  498.1 7.8 %fusion.72 = f32[2,64,2,8]{1,3,0,2:T(8,128)S(1)} fusion(f32[2,2048,2,64,8]{1,3,4,2,0:T(8,128)} %get-tuple-element.172, f32[2,64,2,8]{1,3,0,2:T(8,128)S(1)} %get-tuple-element.173, pred[2,2048]{1,0:T(4,128)(4,1)S(1)} %compare_bitcast_fusion.2), kind=kLoop, calls=%fused_computation.7.clone.1 | loop fusion | flops 16775168 | bytes 16797696 | tf_op jit(solution)/shard_map/while/body/eval_jaxpr/vmap()/reduce_sum | solution.py:73
  513.5 7.1 %fusion.70 = (f32[2,64,2,8]{1,3,0,2:T(8,128)S(1)}, f32[2,2048,2,64,8]{1,3,4,2,0:T(8,128)}) fusion(pred[2,2048]{1,0:T(4,128)(4,1)S(1)} %compare_bitcast_fusion.2, bf16[2048,2,128,1,1]{0,2,4,3,1:T(8,128)(2,1)S(1)} %bitcast.152, bf16[2,64,2,8,128]{4,3,2,1,0:T(8,128)(2,1)S(1)} %dynamic-slice_bitcast_fusion.2), kind=kOutput, calls=%fused_computation.9.clone.1 | convolution fusion | flops 1086322688 | bytes 18362368 | tf_op jit(solution)/shard_map/while/body/eval_jaxpr/vmap(tkgd,lkd->tkgl)/dot_general | solution.py:67
  520.7 7.6 %fusion.71 = f32[2,64,2,8,128]{4,1,3,0,2:T(8,128)S(1)} fusion(bf16[2048,2,128,1,1]{0,2,4,3,1:T(8,128)(2,1)S(1)} %bitcast.156, f32[2,2048,2,64,8]{1,3,4,2,0:T(8,128)} %get-tuple-element.172, f32[2,64,2,8]{1,3,0,2:T(8,128)S(1)} %get-tuple-element.173, pred[2,2048]{1,0:T(4,128)(4,1)S(1)} %compare_bitcast_fusion.2), kind=kOutput, calls=%fused_computation.12.clone.1 | convolution fusion | flops 1090519040 | bytes 18886656 | tf_op jit(solution)/shard_map/while/body/eval_jaxpr/vmap(tkgl,lkd->tkgd)/dot_general | solution.py:76
  528.2 7.8 %fusion.72 = f32[2,64,2,8]{1,3,0,2:T(8,128)S(1)} fusion(f32[2,2048,2,64,8]{1,3,4,2,0:T(8,128)} %get-tuple-element.172, f32[2,64,2,8]{1,3,0,2:T(8,128)S(1)} %get-tuple-element.173, pred[2,2048]{1,0:T(4,128)(4,1)S(1)} %compare_bitcast_fusion.2), kind=kLoop, calls=%fused_computation.7.clone.1 | loop fusion | flops 16775168 | bytes 16797696 | tf_op jit(solution)/shard_map/while/body/eval_jaxpr/vmap()/reduce_sum | solution.py:73
  543.7 7.1 %fusion.70 = (f32[2,64,2,8]{1,3,0,2:T(8,128)S(1)}, f32[2,2048,2,64,8]{1,3,4,2,0:T(8,128)}) fusion(pred[2,2048]{1,0:T(4,128)(4,1)S(1)} %compare_bitcast_fusion.2, bf16[2048,2,128,1,1]{0,2,4,3,1:T(8,128)(2,1)S(1)} %bitcast.152, bf16[2,64,2,8,128]{4,3,2,1,0:T(8,128)(2,1)S(1)} %dynamic-slice_bitcast_fusion.2), kind=kOutput, calls=%fused_computation.9.clone.1 | convolution fusion | flops 1086322688 | bytes 18362368 | tf_op jit(solution)/shard_map/while/body/eval_jaxpr/vmap(tkgd,lkd->tkgl)/dot_general | solution.py:67
  550.8 7.6 %fusion.71 = f32[2,64,2,8,128]{4,1,3,0,2:T(8,128)S(1)} fusion(bf16[2048,2,128,1,1]{0,2,4,3,1:T(8,128)(2,1)S(1)} %bitcast.156, f32[2,2048,2,64,8]{1,3,4,2,0:T(8,128)} %get-tuple-element.172, f32[2,64,2,8]{1,3,0,2:T(8,128)S(1)} %get-tuple-element.173, pred[2,2048]{1,0:T(4,128)(4,1)S(1)} %compare_bitcast_fusion.2), kind=kOutput, calls=%fused_computation.12.clone.1 | convolution fusion | flops 1090519040 | bytes 18886656 | tf_op jit(solution)/shard_map/while/body/eval_jaxpr/vmap(tkgl,lkd->tkgd)/dot_general | solution.py:76
  558.4 7.8 %fusion.72 = f32[2,64,2,8]{1,3,0,2:T(8,128)S(1)} fusion(f32[2,2048,2,64,8]{1,3,4,2,0:T(8,128)} %get-tuple-element.172, f32[2,64,2,8]{1,3,0,2:T(8,128)S(1)} %get-tuple-element.173, pred[2,2048]{1,0:T(4,128)(4,1)S(1)} %compare_bitcast_fusion.2), kind=kLoop, calls=%fused_computation.7.clone.1 | loop fusion | flops 16775168 | bytes 16797696 | tf_op jit(solution)/shard_map/while/body/eval_jaxpr/vmap()/reduce_sum | solution.py:73
  573.9 7.1 %fusion.70 = (f32[2,64,2,8]{1,3,0,2:T(8,128)S(1)}, f32[2,2048,2,64,8]{1,3,4,2,0:T(8,128)}) fusion(pred[2,2048]{1,0:T(4,128)(4,1)S(1)} %compare_bitcast_fusion.2, bf16[2048,2,128,1,1]{0,2,4,3,1:T(8,128)(2,1)S(1)} %bitcast.152, bf16[2,64,2,8,128]{4,3,2,1,0:T(8,128)(2,1)S(1)} %dynamic-slice_bitcast_fusion.2), kind=kOutput, calls=%fused_computation.9.clone.1 | convolution fusion | flops 1086322688 | bytes 18362368 | tf_op jit(solution)/shard_map/while/body/eval_jaxpr/vmap(tkgd,lkd->tkgl)/dot_general | solution.py:67
  581.0 7.6 %fusion.71 = f32[2,64,2,8,128]{4,1,3,0,2:T(8,128)S(1)} fusion(bf16[2048,2,128,1,1]{0,2,4,3,1:T(8,128)(2,1)S(1)} %bitcast.156, f32[2,2048,2,64,8]{1,3,4,2,0:T(8,128)} %get-tuple-element.172, f32[2,64,2,8]{1,3,0,2:T(8,128)S(1)} %get-tuple-element.173, pred[2,2048]{1,0:T(4,128)(4,1)S(1)} %compare_bitcast_fusion.2), kind=kOutput, calls=%fused_computation.12.clone.1 | convolution fusion | flops 1090519040 | bytes 18886656 | tf_op jit(solution)/shard_map/while/body/eval_jaxpr/vmap(tkgl,lkd->tkgd)/dot_general | solution.py:76
  588.5 7.8 %fusion.72 = f32[2,64,2,8]{1,3,0,2:T(8,128)S(1)} fusion(f32[2,2048,2,64,8]{1,3,4,2,0:T(8,128)} %get-tuple-element.172, f32[2,64,2,8]{1,3,0,2:T(8,128)S(1)} %get-tuple-element.173, pred[2,2048]{1,0:T(4,128)(4,1)S(1)} %compare_bitcast_fusion.2), kind=kLoop, calls=%fused_computation.7.clone.1 | loop fusion | flops 16775168 | bytes 16797696 | tf_op jit(solution)/shard_map/while/body/eval_jaxpr/vmap()/reduce_sum | solution.py:73
  604.0 7.1 %fusion.70 = (f32[2,64,2,8]{1,3,0,2:T(8,128)S(1)}, f32[2,2048,2,64,8]{1,3,4,2,0:T(8,128)}) fusion(pred[2,2048]{1,0:T(4,128)(4,1)S(1)} %compare_bitcast_fusion.2, bf16[2048,2,128,1,1]{0,2,4,3,1:T(8,128)(2,1)S(1)} %bitcast.152, bf16[2,64,2,8,128]{4,3,2,1,0:T(8,128)(2,1)S(1)} %dynamic-slice_bitcast_fusion.2), kind=kOutput, calls=%fused_computation.9.clone.1 | convolution fusion | flops 1086322688 | bytes 18362368 | tf_op jit(solution)/shard_map/while/body/eval_jaxpr/vmap(tkgd,lkd->tkgl)/dot_general | solution.py:67
  611.1 7.6 %fusion.71 = f32[2,64,2,8,128]{4,1,3,0,2:T(8,128)S(1)} fusion(bf16[2048,2,128,1,1]{0,2,4,3,1:T(8,128)(2,1)S(1)} %bitcast.156, f32[2,2048,2,64,8]{1,3,4,2,0:T(8,128)} %get-tuple-element.172, f32[2,64,2,8]{1,3,0,2:T(8,128)S(1)} %get-tuple-element.173, pred[2,2048]{1,0:T(4,128)(4,1)S(1)} %compare_bitcast_fusion.2), kind=kOutput, calls=%fused_computation.12.clone.1 | convolution fusion | flops 1090519040 | bytes 18886656 | tf_op jit(solution)/shard_map/while/body/eval_jaxpr/vmap(tkgl,lkd->tkgd)/dot_general | solution.py:76
  618.7 7.8 %fusion.72 = f32[2,64,2,8]{1,3,0,2:T(8,128)S(1)} fusion(f32[2,2048,2,64,8]{1,3,4,2,0:T(8,128)} %get-tuple-element.172, f32[2,64,2,8]{1,3,0,2:T(8,128)S(1)} %get-tuple-element.173, pred[2,2048]{1,0:T(4,128)(4,1)S(1)} %compare_bitcast_fusion.2), kind=kLoop, calls=%fused_computation.7.clone.1 | loop fusion | flops 16775168 | bytes 16797696 | tf_op jit(solution)/shard_map/while/body/eval_jaxpr/vmap()/reduce_sum | solution.py:73
  (214 shorter events, 118.5 us)
Async XLA Ops:
  6.5 46.8 %all-gather.12.cloned.1.call-start = ((), (), s32[]{:S(2)}) async-start(), calls=%async_computation.3 | async-start | bytes 2359296 | tf_op jit(solution)/shard_map/all_gather | solution.py:131
  7.3 63.8 %all-gather.14.cloned.1.call-start = ((), (), s32[]{:S(2)}) async-start(), calls=%async_computation.4 | async-start | bytes 2359296 | tf_op jit(solution)/shard_map/all_gather | solution.py:136
  8.0 1.9 copy-start.7
  8.0 215.2 %all-gather.10.cloned.1.call-start = ((), (), s32[]{:S(2)}) async-start(), calls=%async_computation.2 | async-start | bytes 18874368 | tf_op jit(solution)/shard_map/all_gather | solution.py:126
  8.8 4.4 copy-start.18
  8.8 5.4 copy-start
  8.8 296.3 %all-gather.8.cloned.1.call-start = ((), (), s32[]{:S(2)}) async-start(), calls=%async_computation.1 | async-start | bytes 9437184 | tf_op jit(solution)/shard_map/all_gather | solution.py:181
  9.3 377.8 %all-gather.6.cloned.1.call-start = ((), (), s32[]{:S(2)}) async-start(), calls=%async_computation | async-start | bytes 9437184 | tf_op jit(solution)/shard_map/all_gather | solution.py:182
  10.2 14.9 %collective-permute-start = (bf16[1,256,1024]{1,2,0:T(8,128)(2,1)S(1)}, bf16[1,256,1024]{1,2,0:T(8,128)(2,1)S(1)}, u32[]{:S(2)}, u32[]{:S(2)}) collective-permute-start(bf16[1,256,1024]{1,2,0:T(8,128)(2,1)S(1)} %bitcast.164), channel_id=1, source_target_pairs={{0,8},{8,0},{16,24},{24,16},{1,9},{9,1},{17,25},{25,17},{2,10},{10... | collective-permute-start | bytes 1572872 | tf_op jit(solution)/shard_map/ppermute | solution.py:30
  13.4 14.7 %copy-start.12 = (pred[4]{0:T(512)(128)(4,1)}, pred[4]{0:T(512)(128)(4,1)S(1)}, u32[]{:S(2)}) copy-start(pred[4]{0:T(512)(128)(4,1)S(1)} %get-tuple-element.96) | copy-start | bytes 16
  13.4 15.5 %copy-start.14 = (pred[4]{0:T(512)(128)(4,1)}, pred[4]{0:T(512)(128)(4,1)S(1)}, u32[]{:S(2)}) copy-start(pred[4]{0:T(512)(128)(4,1)S(1)} %get-tuple-element.98) | copy-start | bytes 16
  26.2 24.7 %collective-permute-start.1 = (bf16[2,256,1024]{1,2,0:T(8,128)(2,1)}, bf16[2,256,1024]{1,2,0:T(8,128)(2,1)S(1)}, u32[]{:S(2)}, u32[]{:S(2)}) collective-permute-start(bf16[2,256,1024]{1,2,0:T(8,128)(2,1)} %pad_maximum_fusion), channel_id=1, source_target_pairs={{0,16},{8,24},{16,0},{24,8},{1,17},{9,25},{17,1},{25,9},{2,18},{10... | collective-permute-start | bytes 3145736 | tf_op jit(solution)/shard_map/ppermute | solution.py:30
  53.3 17.7 %copy-start.20 = (f32[256]{0:T(256)S(1)}, f32[256]{0:T(256)}, u32[]{:S(2)}) copy-start(f32[256]{0:T(256)} %param.23) | copy-start | bytes 3076
  55.9 167.4 %copy-start.11 = (f32[2048]{0:T(1024)S(1)}, f32[2048]{0:T(1024)}, u32[]{:S(2)}) copy-start(f32[2048]{0:T(1024)} %param.21) | copy-start | bytes 24580
  232.5 2.0 copy-start.5
  236.9 1.4 copy-start.2
  246.5 3.0 copy-start.3
  250.0 137.1 %copy-start.8 = (f32[8,2,64,16]{2,3,1,0:T(8,128)S(1)}, f32[8,2,64,16]{2,3,1,0:T(8,128)}, u32[]{:S(2)}) copy-start(f32[8,2,64,16]{2,3,1,0:T(8,128)} %custom-call.12) | copy-start | bytes 196612
  250.0 137.1 %copy-start.9 = (f32[8,2,64,16]{2,3,1,0:T(8,128)S(1)}, f32[8,2,64,16]{2,3,1,0:T(8,128)}, u32[]{:S(2)}) copy-start(f32[8,2,64,16]{2,3,1,0:T(8,128)} %custom-call.11) | copy-start | bytes 196612
  392.9 7.1 %copy-start.1 = (bf16[1,2048,256]{1,2,0:T(8,128)(2,1)S(1)}, bf16[1,2048,256]{1,2,0:T(8,128)(2,1)}, u32[]{:S(2)}) copy-start(bf16[1,2048,256]{1,2,0:T(8,128)(2,1)} %copy.164) | copy-start | bytes 3145732 | tf_op jit(solution)/shard_map/while
  423.1 7.1 %copy-start.1 = (bf16[1,2048,256]{1,2,0:T(8,128)(2,1)S(1)}, bf16[1,2048,256]{1,2,0:T(8,128)(2,1)}, u32[]{:S(2)}) copy-start(bf16[1,2048,256]{1,2,0:T(8,128)(2,1)} %copy.164) | copy-start | bytes 3145732 | tf_op jit(solution)/shard_map/while
  453.2 7.1 %copy-start.1 = (bf16[1,2048,256]{1,2,0:T(8,128)(2,1)S(1)}, bf16[1,2048,256]{1,2,0:T(8,128)(2,1)}, u32[]{:S(2)}) copy-start(bf16[1,2048,256]{1,2,0:T(8,128)(2,1)} %copy.164) | copy-start | bytes 3145732 | tf_op jit(solution)/shard_map/while
  483.4 7.1 %copy-start.1 = (bf16[1,2048,256]{1,2,0:T(8,128)(2,1)S(1)}, bf16[1,2048,256]{1,2,0:T(8,128)(2,1)}, u32[]{:S(2)}) copy-start(bf16[1,2048,256]{1,2,0:T(8,128)(2,1)} %copy.164) | copy-start | bytes 3145732 | tf_op jit(solution)/shard_map/while
  513.5 7.1 %copy-start.1 = (bf16[1,2048,256]{1,2,0:T(8,128)(2,1)S(1)}, bf16[1,2048,256]{1,2,0:T(8,128)(2,1)}, u32[]{:S(2)}) copy-start(bf16[1,2048,256]{1,2,0:T(8,128)(2,1)} %copy.164) | copy-start | bytes 3145732 | tf_op jit(solution)/shard_map/while
  543.7 7.1 %copy-start.1 = (bf16[1,2048,256]{1,2,0:T(8,128)(2,1)S(1)}, bf16[1,2048,256]{1,2,0:T(8,128)(2,1)}, u32[]{:S(2)}) copy-start(bf16[1,2048,256]{1,2,0:T(8,128)(2,1)} %copy.164) | copy-start | bytes 3145732 | tf_op jit(solution)/shard_map/while
  573.9 7.1 %copy-start.1 = (bf16[1,2048,256]{1,2,0:T(8,128)(2,1)S(1)}, bf16[1,2048,256]{1,2,0:T(8,128)(2,1)}, u32[]{:S(2)}) copy-start(bf16[1,2048,256]{1,2,0:T(8,128)(2,1)} %copy.164) | copy-start | bytes 3145732 | tf_op jit(solution)/shard_map/while
  604.0 7.1 %copy-start.1 = (bf16[1,2048,256]{1,2,0:T(8,128)(2,1)S(1)}, bf16[1,2048,256]{1,2,0:T(8,128)(2,1)}, u32[]{:S(2)}) copy-start(bf16[1,2048,256]{1,2,0:T(8,128)(2,1)} %copy.164) | copy-start | bytes 3145732 | tf_op jit(solution)/shard_map/while
  629.1 4.9 copy-start.13
  629.1 4.9 copy-start.15
  635.7 1.6 copy-start.6
  635.8 1.6 copy-start.16
  635.8 1.6 copy-start.17
  (3 other events, 3.1 us)
Sparse Core Ops, SparseCore 0:
  9.0 31.7 all-gather.11
  42.4 28.5 all-gather.13
  72.6 150.5 all-gather.9
  224.7 80.2 all-gather.7
  306.5 80.5 all-gather.5
